TPU v7x, 256 devices: a whole 4x4x8 slice. The times are simulated.
256 devices in a mesh: req: 32 (over z, x), row: 2 (over core), col: 4 (over y).
Axes of the slice: x: 4, y: 4, z: 8, core: 2. Of those that a mesh axis runs over, the one named last changes fastest.
Arguments:
- tokens: bfloat16 [32768, 1024], P(('req', 'row'), 'col'), may hold values from -6 to 6
- w_proj: bfloat16 [1024, 8, 512], P('col', 'row'), may hold values from -0.1875 to 0.1875
- adapter_a: bfloat16 [64, 1024, 16], P('req'), may hold values from -0.1875 to 0.1875
- adapter_b: bfloat16 [64, 16, 8, 256], P('req', None, 'row'), may hold values from -0.8984375 to 0.8984375
- adapter_row: int32 [64], replicated, may hold values from 0 to 63, each once
- adapter_of: int32 [32, 2], replicated, may hold values from 0 to 63
- len_blocks: int32 [32, 2], replicated, may hold values from 1 to 12, 16 in all within a row
- state_slot: int32 [64], replicated, may hold values from 0 to 63, as said below
- init_state: float32 [64, 8, 128, 128], P('req', 'row'), may hold values from -3 to 3
- decay: float32 [512, 8], P(('req', 'col'), 'row'), may hold values from 0 to 1, as said below
Outputs:
- memory_out: bfloat16 [32768, 1024], P(('req', 'col'), 'row')
Inputs may be any that keep to these rules, and one draw needn't show every extreme that they name: `len_blocks`: each row sums to 16. `state_slot`: a permutation of the slots; slots k * 2 to (k + 1) * 2 - 1 are those of req index k. The 2 requests of req index g take one slot of req index (g - 1) mod 32 and one of req index (g - 16) mod 32, in an order and at positions within those indices that vary by draw. `decay`: every factor is above 0 and at most 1.
All inputs are finite; a program needn't handle non-finite values.
Results may differ from a plain program's by a relative error of at most 0.0062.
Values may be sent and summed in bfloat16 or wider, within the bound.
A program may use at most 128 MiB of HBM per device.

v0:
```python
import math
import jax
import jax.numpy as jnp
from jax import lax
from jax.sharding import PartitionSpec as P

BLK = 64


def carried_in(value, axis, join, neutral):
    place = lax.axis_index(axis)
    gathered = jax.tree.map(
        lambda a, kind: lax.all_gather(a.astype(kind), axis),
        value,
        jax.tree.map(lambda a: jnp.bfloat16 if a.dtype == jnp.float32 else a.dtype, value),
    )
    state = jax.tree.map(lambda a, e: jnp.zeros_like(a) + jnp.asarray(e, a.dtype), value, neutral)

    def one(lap, state):
        return join(
            state,
            jax.tree.map(
                lambda a, own: lax.dynamic_index_in_dim(a, lap, 0, False).astype(own.dtype),
                gathered,
                value,
            ),
        )

    return lax.fori_loop(0, place, one, state)


def unit(values):
    scale = lax.rsqrt(jnp.mean(values * values, axis=-1, keepdims=True) + 1e-06)
    return values * scale / math.sqrt(values.shape[-1])


def block_info(lengths, block_ids):
    starts = jnp.cumsum(lengths) - lengths
    is_start = jnp.any(block_ids[:, None] == starts[None, :], axis=1)
    request = jnp.sum((block_ids[:, None] >= starts[None, :]).astype(jnp.int32), axis=1) - 1
    return (is_start, request)


def add_adapter(base_part, delta):
    return jnp.stack(
        [
            base_part[:, :, 0] + delta[:, :, 0],
            base_part[:, :, 1],
            base_part[:, :, 2] + delta[:, :, 1],
            base_part[:, :, 3],
        ],
        axis=2,
    )


def compose(earlier, later):
    return (earlier[0] * later[0], later[0][:, None, None] * earlier[1] + later[1])


def body(
    tokens,
    w_proj,
    adapter_a,
    adapter_b,
    adapter_row,
    adapter_of,
    len_blocks,
    state_slot,
    init_state,
    decay,
):
    highest = lax.Precision.HIGHEST
    group_id = lax.axis_index("req")
    column = lax.axis_index("col")
    n_col = lax.axis_size("col")
    width = adapter_a.shape[1]
    rank = adapter_a.shape[2]
    req_grp = adapter_of.shape[1]
    heads_here = w_proj.shape[1]
    head_dim = w_proj.shape[2] // 4
    slice_width = tokens.shape[1]
    gathered = lax.all_gather(tokens, "row", axis=0, tiled=True)
    group_tok = gathered.shape[0]
    own_count = group_tok // n_col
    nblk_group = group_tok // BLK
    nblk_here = own_count // BLK
    block_ids = jnp.arange(nblk_group, dtype=jnp.int32)
    is_start, request = block_info(len_blocks[group_id], block_ids)
    onehot = (
        jnp.repeat(request, BLK)[:, None] == jnp.arange(req_grp, dtype=jnp.int32)[None, :]
    ).astype(jnp.float32)
    picked = adapter_row[adapter_of[group_id]]
    table_a, table_b = (
        lax.all_gather(adapter_a, "req", axis=0, tiled=True),
        lax.all_gather(adapter_b, "req", axis=0, tiled=True),
    )
    chosen_a = table_a[picked]
    chosen_b = table_b[picked]
    a_stack = jnp.transpose(chosen_a, (1, 0, 2)).reshape(width, req_grp * rank)
    b_stack = chosen_b.reshape(req_grp * rank, heads_here * 2 * head_dim).astype(jnp.float32)
    w_flat = w_proj.reshape(w_proj.shape[0], heads_here * 4 * head_dim)
    a_part = lax.dynamic_slice_in_dim(a_stack, column * slice_width, slice_width, 0)
    count = own_count * lax.axis_size("col")
    projected = jnp.dot(gathered, w_flat, preferred_element_type=jnp.float32)
    lowrank = jnp.dot(gathered, a_part, preferred_element_type=jnp.float32).reshape(
        count, req_grp, rank
    )
    lowrank = (lowrank * onehot[:, :, None]).reshape(count, req_grp * rank)
    delta = jnp.dot(lowrank, b_stack, precision=highest)
    joined = add_adapter(
        projected.reshape(count, heads_here, 4, head_dim),
        delta.reshape(count, heads_here, 2, head_dim),
    )
    summed = lax.psum_scatter(
        joined.reshape(count, heads_here * 4 * head_dim), "col", scatter_dimension=0, tiled=True
    )
    parts = summed.reshape(own_count, heads_here, 4, head_dim).astype(jnp.bfloat16)
    here_start = lax.dynamic_slice_in_dim(is_start, column * nblk_here, nblk_here, 0)
    here_request = lax.dynamic_slice_in_dim(request, column * nblk_here, nblk_here, 0)
    state_table = lax.all_gather(init_state, "req", axis=0, tiled=True)
    state_index = state_slot[group_id * req_grp + here_request]
    query = unit(parts[:, :, 0].astype(jnp.float32)).reshape(nblk_here, BLK, heads_here, head_dim)
    keys_n = unit(parts[:, :, 1].astype(jnp.float32)).reshape(nblk_here, BLK, heads_here, head_dim)
    values = parts[:, :, 2].astype(jnp.float32).reshape(nblk_here, BLK, heads_here, head_dim)
    causal = jnp.tril(jnp.ones((BLK, BLK), jnp.float32))

    def step(carry, blocks):
        amount, state = carry
        q_block, k_block, v_block, fade, start_here, slot = blocks
        amount = jnp.where(start_here, jnp.zeros_like(amount), amount)
        state = jnp.where(start_here, state_table[slot], state)
        read = jnp.einsum("thd,hde->the", q_block, state, precision=highest)
        scores = jnp.einsum("thd,shd->hts", q_block, k_block, precision=highest) * causal[None]
        inner = jnp.einsum("hts,she->the", scores, v_block, precision=highest)
        update = jnp.einsum("thd,the->hde", k_block, v_block, precision=highest) / BLK
        return ((fade * amount, fade[:, None, None] * state + update), (read + inner, amount))

    start_carry = (
        jnp.ones((heads_here,), jnp.float32),
        jnp.zeros((heads_here, head_dim, head_dim), jnp.float32),
    )
    last_carry, (local_mem, amounts) = lax.scan(
        step, start_carry, (query, keys_n, values, decay, here_start, state_index)
    )
    identity = (
        jnp.ones((heads_here,), jnp.float32),
        jnp.zeros((heads_here, head_dim, head_dim), jnp.float32),
    )
    incoming = carried_in(last_carry, "col", compose, identity)
    carried = jnp.einsum("nthd,hde->nthe", query, incoming[1], precision=highest)
    mem = local_mem + carried * amounts[:, None, :, None]
    gate_part = parts[:, :, 3].astype(jnp.float32)
    result = jax.nn.sigmoid(gate_part) * mem.reshape(own_count, heads_here, head_dim)
    return result.reshape(own_count, heads_here * head_dim).astype(jnp.bfloat16)


def solution(mesh):
    placed = (
        P(("req", "row"), "col"),
        P("col", "row", None),
        P("req", None, None),
        P("req", None, "row", None),
        P(),
        P(),
        P(),
        P(),
        P("req", "row", None, None),
        P(("req", "col"), "row"),
    )
    return jax.shard_map(
        body, mesh=mesh, in_specs=placed, out_specs=P(("req", "col"), "row"), check_vma=False
    )
```

profile of v0, /device:TPU:2, one launch (start us, length us, event | category | flops | bytes accessed | tf_op | source)
XLA Modules:
  0.0 471.5 jit_solution(1949894486857903738)
XLA Ops:
  10.1 1.5 copy.92
  12.9 2.2 all_gather.24
  15.1 4.5 fusion.29
  19.6 70.0 %all-gather.8.cloned.1.call-done = bf16[64,16,4,256]{3,1,2,0:T(8,128)(2,1)} async-done(((bf16[2,16,4,256]{3,1,2,0:T(8,128)(2,1)}), bf16[64,16,4,256]{3,1,2,0:T(8,128)(2,1)}) %all-gather.8.cloned.1.call-update) | async-done | bytes 2097168 | tf_op jit(solution)/shard_map/all_gather | solution.py:95
  89.6 2.1 gather_fusion.2
  91.8 75.5 %all-gather.6.cloned.1.call-done = bf16[64,1024,16]{1,2,0:T(8,128)(2,1)} async-done(((bf16[2,1024,16]{1,2,0:T(8,128)(2,1)}), bf16[64,1024,16]{1,2,0:T(8,128)(2,1)}) %all-gather.6.cloned.1.call-update) | async-done | bytes 2097168 | tf_op jit(solution)/shard_map/all_gather | solution.py:94
  167.3 2.1 gather_fusion.1
  169.7 1.9 fusion.32
  171.6 5.0 %slice_add_fusion.1 = (f32[1024,4,1,128]{0,3,2,1:T(8,128)S(1)}, f32[1024,4,1,128]{0,3,2,1:T(8,128)S(1)}, f32[1024,4,1,128]{0,3,2,1:T(8,128)S(1)}, f32[1024,4,1,128]{0,3,2,1:T(8,128)S(1)}) fusion(f32[1024,4,2,128]{0,3,2,1:T(8,128)S(1)} %fusion.32, f32[1024,4,4,128]{0,3,2,1:T(8,128)} %fusion.29), kind=kLoop, calls=%fused_computation.42 | loop fusion | flops 1048576 | bytes 20971520 | tf_op jit(solution)/shard_map/add | solution.py:47
  176.7 3.6 pad_maximum_fusion
  183.0 79.0 %reduce-scatter.2.cloned.1.call-done = f32[256,2048]{0,1:T(8,128)} async-done(((f32[1024,2048]{0,1:T(8,128)}), f32[256,2048]{0,1:T(8,128)}) %reduce-scatter.2.cloned.1.call-update) | async-done | bytes 2097168 | tf_op jit(solution)/shard_map/reduce_scatter | solution.py:114
  262.0 1.7 convert_element_type.78
  265.3 137.4 %all-gather.10.cloned.1.call-done = f32[64,4,128,128]{3,2,1,0:T(8,128)} async-done(((f32[2,4,128,128]{3,2,1,0:T(8,128)}), f32[64,4,128,128]{3,2,1,0:T(8,128)}) %all-gather.10.cloned.1.call-update) | async-done | bytes 16777232 | tf_op jit(solution)/shard_map/all_gather | solution.py:120
  402.6 35.4 %while.30 = (s32[]{:T(128)}, f32[4]{0:T(128)S(1)}, f32[4,128,128]{2,1,0:T(8,128)S(1)}, f32[4,64,4,128]{3,1,0,2:T(8,128)S(1)}, f32[4,4]{1,0:T(4,128)S(1)}, /*inde...) while((s32[]{:T(128)}, f32[4]{0:T(128)S(1)}, ...), condition=%wide.region_7.8_spmd.clone, body=%wide.region_6.7_spmd.clone.sunk | while | flops 151511056 | bytes 2741074 | solution.py:142
  406.1 1.9 fusion.70
  409.3 2.1 fusion.67
  415.0 1.9 fusion.70
  418.1 2.1 fusion.67
  423.8 1.9 fusion.70
  427.0 2.1 fusion.67
  432.7 1.9 fusion.70
  435.8 2.1 fusion.67
  438.3 13.3 %all-gather.1 = bf16[16,128,128]{2,1,0:T(8,128)(2,1)S(1)} all-gather(bf16[4,128,128]{2,1,0:T(8,128)(2,1)S(1)} %convert_element_type.90), channel_id=3, replica_groups=mesh['req'=32,'row'=2,'col'=4] {'col'}, dimensions={0}, use_global_device_ids=true | all-gather | bytes 655360 | tf_op jit(solution)/shard_map/all_gather | solution.py:13
  451.6 10.4 %all-reduce = bf16[16]{0:T(256)(128)(2,1)S(1)} all-reduce(bf16[16]{0:T(256)(128)(2,1)S(1)} %dynamic-update-slice), channel_id=2, replica_groups=mesh['req'=32,'row'=2,'col'=4] {'col'}, use_global_device_ids=true, to_apply=%add | all-reduce | flops 16 | bytes 64
  (101 shorter events, 24.2 us)
Async XLA Ops:
  6.5 174.6 %copy-start = (s32[64]{0:T(128)S(1)}, s32[64]{0:T(128)}, u32[]{:S(2)}) copy-start(s32[64]{0:T(128)} %param.21) | copy-start | bytes 772
  6.5 83.0 %all-gather.8.cloned.1.call-start = ((), (), s32[]{:S(2)}) async-start(), calls=%async_computation.2 | async-start | bytes 2162688 | tf_op jit(solution)/shard_map/all_gather | solution.py:95
  8.1 159.3 %all-gather.6.cloned.1.call-start = ((), (), s32[]{:S(2)}) async-start(), calls=%async_computation.1 | async-start | bytes 2162688 | tf_op jit(solution)/shard_map/all_gather | solution.py:94
  8.8 253.2 %reduce-scatter.2.cloned.1.call-start = ((), (), s32[]{:S(2)}) async-start(), calls=%async_computation.3 | async-start | bytes 10485760 | tf_op jit(solution)/shard_map/reduce_scatter | solution.py:114
  10.1 2.1 copy-start.1
  10.1 2.8 copy-start.3
  180.2 1.5 copy-start.4
  180.3 222.4 %all-gather.10.cloned.1.call-start = ((), (), s32[]{:S(2)}) async-start(), calls=%async_computation.4 | async-start | bytes 17301504 | tf_op jit(solution)/shard_map/all_gather | solution.py:120
  264.4 138.3 %copy-start.2 = (f32[4,64,4,128]{3,1,0,2:T(8,128)S(1)}, f32[4,64,4,128]{3,1,0,2:T(8,128)}, u32[]{:S(2)}) copy-start(f32[4,64,4,128]{3,1,0,2:T(8,128)} %custom-call.10) | copy-start | bytes 1572868
Sparse Core Ops, SparseCore 0:
  9.9 79.6 all-gather.7
  92.1 75.1 all-gather.5
  180.4 81.5 reduce-scatter.1
  264.4 138.1 all-gather.9
where the time goes:
time: 472 us
  waiting for transfers between devices  363 us (77%)
  blocking collectives  25.9 us (5%)
  matrix products  25.8 us (5%)
  local copies, waits for them, and re-layouts  18.8 us (4%)
  other arithmetic  16.8 us (4%)
  between operations  14 us (3%)
  loops' own time  6.94 us (1%)
    all_gather x1, waiting for transfers between devices, body(): state_table = lax.all_gather(init_state, 'req', axis=0, tiled=True)  137 us
    reduce_scatter x1, waiting for transfers between devices, body(): lax.psum_scatter(joined.reshape(count, heads_here * 4 * head_dim), 'col',...  79 us
    all_gather x1, waiting for transfers between devices, body(): lax.all_gather(adapter_a, 'req', axis=0, tiled=True)  75.5 us
    all_gather x1, waiting for transfers between devices, body(): lax.all_gather(adapter_b, 'req', axis=0, tiled=True)  70 us
    all_gather x1, blocking collectives, carried_in(): lax.all_gather(a.astype(kind), axis)  13.3 us
    unnamed x1, blocking collectives  10.4 us
  transfers between devices with their start and end apart: 4, of which 4 were waited for; matrix products, arithmetic and copies ran while one was open for 3% of the time, Pallas kernels for 0%

commit v1 on v0

--- a/solution.py
+++ b/solution.py
@@ -117,7 +117,13 @@
     parts = summed.reshape(own_count, heads_here, 4, head_dim).astype(jnp.bfloat16)
     here_start = lax.dynamic_slice_in_dim(is_start, column * nblk_here, nblk_here, 0)
     here_request = lax.dynamic_slice_in_dim(request, column * nblk_here, nblk_here, 0)
-    state_table = lax.all_gather(init_state, "req", axis=0, tiled=True)
+    arrivals = []
+    for _ in range(jax.lax.axis_size("req")):
+        arrivals.append(init_state)
+    f_now = jnp.stack(arrivals, 0)
+    state_table = jnp.concatenate(
+        jax.lax.all_to_all(f_now, axis_name="req", split_axis=0, concat_axis=0), 0
+    )
     state_index = state_slot[group_id * req_grp + here_request]
     query = unit(parts[:, :, 0].astype(jnp.float32)).reshape(nblk_here, BLK, heads_here, head_dim)
     keys_n = unit(parts[:, :, 1].astype(jnp.float32)).reshape(nblk_here, BLK, heads_here, head_dim)

time: 472 us -> 631 us (1.34)
  waiting for transfers between devices: 363 us -> 502 us
  starting transfers between devices: 0.12 us -> 11.9 us
  local copies, waits for them, and re-layouts: 18.8 us -> 25.7 us
    all_gather x1, waiting for transfers between devices: 75.5 us -> 230 us  [body(): lax.all_gather(adapter_a, 'req', axis=0, tiled=True)]
    all_gather x1 -> x0, waiting for transfers between devices: 137 us -> none  [body(): state_table = lax.all_gather(init_state, 'req', axis=0, tiled=True)]
    all_gather x1, waiting for transfers between devices: 70 us -> 187 us  [body(): lax.all_gather(adapter_b, 'req', axis=0, tiled=True)]
    all_to_all x0 -> x1, starting transfers between devices: none -> 11.8 us  [body(): jax.lax.all_to_all(f_now, axis_name='req', split_axis=0, concat_axis=0)]
    another operation x1 -> x2, local copies, waits for them, and re-layouts: 0.02 us -> 8.93 us  [the longest x1 8.91 us: body(): f_now = jnp.stack(arrivals, 0)]
  transfers between devices with their start and end apart: 4 -> 4, of which waited for: 4 -> 3; matrix products, arithmetic and copies ran while one was open for 3% -> 4% of each run, Pallas kernels for 0% -> 0%
where the time goes in v1:
time: 631 us; the launch traced here: 630 us
  waiting for transfers between devices  502 us (80%)
  matrix products  26.8 us (4%)
  local copies, waits for them, and re-layouts  25.7 us (4%)
  blocking collectives  23.5 us (4%)
  other arithmetic  17.3 us (3%)
  between operations  14 us (2%)
  starting transfers between devices  11.9 us (2%)
  loops' own time  8.46 us (1%)
    all_gather x1, waiting for transfers between devices, body(): lax.all_gather(adapter_a, 'req', axis=0, tiled=True)  230 us
    all_gather x1, waiting for transfers between devices, body(): lax.all_gather(adapter_b, 'req', axis=0, tiled=True)  187 us
    reduce_scatter x1, waiting for transfers between devices, body(): lax.psum_scatter(joined.reshape(count, heads_here * 4 * head_dim), 'col',...  84.8 us
    all_gather x1, blocking collectives, carried_in(): lax.all_gather(a.astype(kind), axis)  13.4 us
  transfers between devices with their start and end apart: 4, of which 3 were waited for; matrix products, arithmetic and copies ran while one was open for 4% of the time, Pallas kernels for 0%

profile of v1, /device:TPU:2, one launch (start us, length us, event | category | flops | bytes accessed | tf_op | source)
XLA Modules:
  0.0 629.5 jit_solution(12986283949152098226)
XLA Ops:
  6.5 8.9 %stack.5 = f32[32,2,4,128,128]{4,3,2,1,0:T(8,128)} broadcast(f32[2,4,128,128]{3,2,1,0:T(8,128)} %param.22), dimensions={1,2,3,4} | broadcast | bytes 17301504 | tf_op jit(solution)/shard_map/stack | solution.py:123
  15.5 11.8 %all-to-all-start = ((f32[32,2,4,128,128]{4,3,2,1,0:T(8,128)}), f32[32,2,4,128,128]{4,3,2,1,0:T(8,128)}, u32[]{:S(2)}, u32[]{:S(2)}) async-start(f32[32,2,4,128,128]{4,3,2,1,0:T(8,128)} %stack.5), calls=%async_computation.1 | async-start | bytes 33554432 | tf_op jit(solution)/shard_map/all_to_all | solution.py:125
  30.9 2.2 all_gather.21
  33.1 4.5 fusion.29
  37.6 186.7 %all-gather.7.cloned.1.call-done = bf16[64,16,4,256]{3,1,2,0:T(8,128)(2,1)} async-done(((bf16[2,16,4,256]{3,1,2,0:T(8,128)(2,1)}), bf16[64,16,4,256]{3,1,2,0:T(8,128)(2,1)}) %all-gather.7.cloned.1.call-update) | async-done | bytes 2097168 | tf_op jit(solution)/shard_map/all_gather | solution.py:95
  224.3 2.1 gather_fusion.2
  226.5 229.7 %all-gather.5.cloned.1.call-done = bf16[64,1024,16]{1,2,0:T(8,128)(2,1)} async-done(((bf16[2,1024,16]{1,2,0:T(8,128)(2,1)}), bf16[64,1024,16]{1,2,0:T(8,128)(2,1)}) %all-gather.5.cloned.1.call-update) | async-done | bytes 2097168 | tf_op jit(solution)/shard_map/all_gather | solution.py:94
  456.2 2.1 gather_fusion.1
  458.6 1.9 fusion.32
  460.5 5.0 slice_add_fusion.1
  465.6 3.5 pad_maximum_fusion
  471.2 84.8 %reduce-scatter.2.cloned.1.call-done = f32[256,2048]{0,1:T(8,128)} async-done(((f32[1024,2048]{0,1:T(8,128)}), f32[256,2048]{0,1:T(8,128)}) %reduce-scatter.2.cloned.1.call-update) | async-done | bytes 2097168 | tf_op jit(solution)/shard_map/reduce_scatter | solution.py:114
  556.0 1.7 convert_element_type.78
  559.4 39.1 %while.30 = (s32[]{:T(128)}, f32[4]{0:T(128)S(1)}, f32[4,128,128]{2,1,0:T(8,128)S(1)}, f32[4,64,4,128]{3,1,0,2:T(8,128)S(1)}, f32[4,4]{1,0:T(4,128)S(1)}, /*inde...) while((s32[]{:T(128)}, f32[4]{0:T(128)S(1)}, ...), condition=%wide.region_7.8_spmd.clone, body=%wide.region_6.7_spmd.clone.sunk | while | flops 151511056 | bytes 2741074 | solution.py:148
  563.4 2.0 fusion.70
  566.8 2.3 fusion.67
  573.2 2.0 fusion.70
  576.6 2.3 fusion.67
  583.0 2.0 fusion.70
  586.4 2.3 fusion.67
  592.8 2.0 fusion.70
  596.2 2.3 fusion.67
  598.8 13.4 %all-gather.1 = bf16[16,128,128]{2,1,0:T(8,128)(2,1)S(1)} all-gather(bf16[4,128,128]{2,1,0:T(8,128)(2,1)S(1)} %convert_element_type.90), channel_id=3, replica_groups=mesh['req'=32,'row'=2,'col'=4] {'col'}, dimensions={0}, use_global_device_ids=true | all-gather | bytes 655360 | tf_op jit(solution)/shard_map/all_gather | solution.py:13
  612.2 7.9 %all-reduce = bf16[16]{0:T(256)(128)(2,1)S(1)} all-reduce(bf16[16]{0:T(256)(128)(2,1)S(1)} %dynamic-update-slice), channel_id=2, replica_groups=mesh['req'=32,'row'=2,'col'=4] {'col'}, use_global_device_ids=true, to_apply=%add | all-reduce | flops 16 | bytes 64
  (109 shorter events, 23.7 us)
Async XLA Ops:
  6.5 462.9 %copy-start = (s32[64]{0:T(128)S(1)}, s32[64]{0:T(128)}, u32[]{:S(2)}) copy-start(s32[64]{0:T(128)} %param.21) | copy-start | bytes 772
  15.4 11.9 %copy-start.5 = (bf16[2,16,4,256]{3,2,1,0:T(4,128)(2,1)S(1)}, bf16[2,16,4,256]{3,2,1,0:T(4,128)(2,1)}, u32[]{:S(2)}) copy-start(bf16[2,16,4,256]{3,2,1,0:T(4,128)(2,1)} %param.17) | copy-start | bytes 196612
  15.5 13.4 %copy-start.6 = (s32[32,2]{0,1:T(2,128)S(1)}, s32[32,2]{0,1:T(2,128)}, u32[]{:S(2)}) copy-start(s32[32,2]{0,1:T(2,128)} %param.19) | copy-start | bytes 772
  15.5 13.4 %copy-start.7 = (s32[32,2]{0,1:T(2,128)S(1)}, s32[32,2]{0,1:T(2,128)}, u32[]{:S(2)}) copy-start(s32[32,2]{0,1:T(2,128)} %param.20) | copy-start | bytes 772
  15.5 14.0 %copy-start.2 = (bf16[256,4,512]{2,1,0:T(4,128)(2,1)S(1)}, bf16[256,4,512]{2,1,0:T(4,128)(2,1)}, u32[]{:S(2)}) copy-start(bf16[256,4,512]{2,1,0:T(4,128)(2,1)} %param.15) | copy-start | bytes 3145732
  15.5 543.8 %all-to-all-start = ((f32[32,2,4,128,128]{4,3,2,1,0:T(8,128)}), f32[32,2,4,128,128]{4,3,2,1,0:T(8,128)}, u32[]{:S(2)}, u32[]{:S(2)}) async-start(f32[32,2,4,128,128]{4,3,2,1,0:T(8,128)} %stack.5), calls=%async_computation.1 | async-start | bytes 33554432 | tf_op jit(solution)/shard_map/all_to_all | solution.py:125
  27.3 197.0 %all-gather.7.cloned.1.call-start = ((), (), s32[]{:S(2)}) async-start(), calls=%async_computation.3 | async-start | bytes 2162688 | tf_op jit(solution)/shard_map/all_gather | solution.py:95
  28.0 428.2 %all-gather.5.cloned.1.call-start = ((), (), s32[]{:S(2)}) async-start(), calls=%async_computation.2 | async-start | bytes 2162688 | tf_op jit(solution)/shard_map/all_gather | solution.py:94
  28.8 527.2 %reduce-scatter.2.cloned.1.call-start = ((), (), s32[]{:S(2)}) async-start(), calls=%async_computation.4 | async-start | bytes 10485760 | tf_op jit(solution)/shard_map/reduce_scatter | solution.py:114
  29.4 0.8 copy-start.1
  29.4 1.5 copy-start.4
  469.1 1.0 copy-start.8
  558.4 1.0 copy-start.3
Sparse Core Ops, SparseCore 0:
  30.7 193.5 all-gather.6
  226.9 229.3 all-gather.4
  469.2 86.6 reduce-scatter.1
